TPU v7x, 256 devices: a whole 4x4x8 slice. The times are simulated.
256 devices in a mesh: rows: 16 (over z, core), cols: 16 (over y, x).
Axes of the slice: x: 4, y: 4, z: 8, core: 2. Of those that a mesh axis runs over, the one named last changes fastest.
Arguments:
- window_slab: float32 [24576, 4096], P('rows', 'cols'), may hold values from -6 to 6
- first_inverse: float32 [2, 512, 512], replicated, may hold values from -2 to 2, as said below
- first_factor: float32 [2, 512, 24576], P(None, 'cols', 'rows'), may hold values from -0.25 to 0.25
- second_inverse: float32 [2, 512, 512], replicated, may hold values from -2 to 2, as said below
- second_factor: float32 [2, 512, 4096], P(None, 'cols', 'rows'), may hold values from -0.25 to 0.25
Outputs:
- reduced: float32 [24576, 4096], P('cols', 'rows')
Inputs may be any that keep to these rules, and one draw needn't show every extreme that they name: first_inverse[k] is lower triangular with diagonal entries from 0.5 to 2. second_inverse[k] is lower triangular with diagonal entries from 0.5 to 2.
All inputs are finite; a program needn't handle non-finite values.
Results may differ from a plain program's by a relative error of at most 0.0001.
Values sent between devices are 32-bit elements; how exact they have to be, the bound alone decides.
A program may use at most 64 MiB of HBM per device.

v0:
```python
import jax
import jax.numpy as jnp
from jax import lax
from jax.sharding import PartitionSpec as P

BLOCK = 128
HIGHEST = lax.Precision.HIGHEST
CONTRACT_ROWS = (((0,), (0,)), ((), ()))
CONTRACT_COLS = (((1,), (1,)), ((), ()))


def right_solve(current, first_column, inverses, total_of, update_of):
    height, breadth = current.shape
    panel_count = inverses.shape[0]
    panel_width = inverses.shape[1]
    portion = min(breadth, panel_width)
    columns = first_column + lax.broadcasted_iota(jnp.int32, (1, breadth), 1)
    for panel_index in range(panel_count):
        panel_start = panel_index * panel_width
        panel_end = panel_start + panel_width
        inner_offset = jnp.clip(first_column - panel_start, 0, panel_width - portion)
        member = jnp.logical_and(first_column < panel_end, first_column + breadth > panel_start)
        own_columns = current
        inverse_cols = lax.dynamic_slice_in_dim(inverses[panel_index], inner_offset, portion, 1)
        partial_value = lax.dot_general(
            own_columns,
            inverse_cols,
            CONTRACT_COLS,
            precision=HIGHEST,
            preferred_element_type=jnp.float32,
        )
        solved = total_of(jnp.where(member, partial_value, 0.0))
        update = update_of(panel_index, solved)
        current = jnp.where(columns >= panel_end, current - update, current)
        mine_cols = lax.dynamic_slice_in_dim(solved, inner_offset, portion, 1)
        present = current
        current = jnp.where(member, mine_cols, present)
    return current


def on_device(window_slab, first_inverse, first_factor, second_inverse, second_factor):
    row_count = lax.axis_size("rows")
    row_index = lax.axis_index("rows")
    row_share, breadth = window_slab.shape
    panel_count = first_inverse.shape[0]
    panel_width = first_inverse.shape[1]
    blocks_per_panel = panel_width // BLOCK
    local_rows = lax.broadcasted_iota(jnp.int32, (row_share, 1), 0)
    logical_rows = (local_rows // BLOCK * row_count + row_index) * BLOCK + local_rows % BLOCK
    current = window_slab
    for panel_index in range(panel_count):
        panel_start = panel_index * panel_width
        panel_end = panel_start + panel_width
        local_block = panel_start // (row_count * BLOCK)
        first_group = panel_start // BLOCK % row_count
        member = jnp.logical_and(
            row_index >= first_group, row_index < first_group + blocks_per_panel
        )
        offset = jnp.clip(row_index - first_group, 0, blocks_per_panel - 1) * BLOCK
        own_rows = current[local_block * BLOCK : (local_block + 1) * BLOCK]
        inverse_cols = lax.dynamic_slice_in_dim(first_inverse[panel_index], offset, BLOCK, 1)
        partial_value = jnp.dot(
            inverse_cols, own_rows, precision=HIGHEST, preferred_element_type=jnp.float32
        )
        solved = lax.psum(jnp.where(member, partial_value, 0.0), "rows")
        update = lax.dot_general(
            lax.all_gather(first_factor[panel_index], "cols", axis=0, tiled=True),
            solved,
            CONTRACT_ROWS,
            precision=HIGHEST,
            preferred_element_type=jnp.float32,
        )
        current = jnp.where(logical_rows >= panel_end, current - update, current)
        mine_rows = lax.dynamic_slice_in_dim(solved, offset, BLOCK, 0)
        present = current[local_block * BLOCK : (local_block + 1) * BLOCK]
        current = lax.dynamic_update_slice_in_dim(
            current, jnp.where(member, mine_rows, present), local_block * BLOCK, 0
        )
    turned = lax.all_to_all(
        lax.all_to_all(current, "cols", split_axis=0, concat_axis=1, tiled=True),
        "rows",
        split_axis=1,
        concat_axis=0,
        tiled=True,
    )
    height, narrow = turned.shape

    def total_rows(partial_sum):
        return lax.psum(partial_sum, "rows")

    def update_rows(panel_number, solved_cols):
        return jnp.dot(
            solved_cols,
            lax.all_gather(second_factor[panel_number], "cols", axis=0, tiled=True),
            precision=HIGHEST,
            preferred_element_type=jnp.float32,
        )

    reduced = right_solve(turned, row_index * narrow, second_inverse, total_rows, update_rows)
    return reduced


def solution(mesh):
    return jax.shard_map(
        on_device,
        mesh=mesh,
        in_specs=(P("rows", "cols"), P(), P(None, "cols", "rows"), P(), P(None, "cols", "rows")),
        out_specs=P("cols", "rows"),
        check_vma=False,
    )
```

profile of v0, /device:TPU:1, one launch (start us, length us, event | category | flops | bytes accessed | tf_op | source)
XLA Modules:
  0.0 586.9 jit_solution(826307015627052051)
XLA Ops:
  7.4 0.0 all-reduce.5.cloned.1.call-start
  7.4 0.0 copy-start.1
  7.4 2.8 fusion.57
  10.2 0.0 copy-start.2
  10.2 0.0 copy-done.1
  10.2 1.4 convolution_select_fusion.3
  11.5 0.0 all-reduce.5.cloned.1.call-update
  11.6 0.0 all-gather.7.cloned.1.call-start
  11.6 0.0 copy-done.2
  11.6 0.8 fusion.58
  12.4 0.0 all-gather.7.cloned.1.call-update
  12.4 0.0 all-gather.9.cloned.1.call-start
  12.5 0.5 all-gather.9.cloned.1.call-update
  13.0 0.0 all-reduce.7.cloned.1.call-start
  13.1 113.7 %all-reduce.5.cloned.1.call-done = f32[512,256]{1,0:T(8,128)} async-done(((f32[512,256]{1,0:T(8,128)}), f32[512,256]{1,0:T(8,128)}) %all-reduce.5.cloned.1.call-update) | async-done | bytes 524304 | tf_op jit(solution)/shard_map/psum | solution.py:65
  126.8 0.0 all-gather.7.cloned.1.call-done
  126.8 7.2 %fusion.14 = f32[1536,256]{1,0:T(8,128)S(1)} fusion(f32[1536,256]{1,0:T(8,128)S(1)} %copy-done.1, f32[512,256]{1,0:T(8,128)} %all-reduce.5.cloned.1.call-done, f32[1,512,1536]{2,1,0:T(8,128)} %all-gather.7.cloned.1.call-done, pred[1536]{0:T(1024)(128)(4,1)S(1)} %broadcast_compare_fusion), kind=kOutput, calls=%fused_computation.14 | convolution fusion | flops 2416705536 | bytes 6817280 | tf_op jit(solution)/shard_map/dot_general | solution.py:66
  134.0 2.4 convolution_select_fusion.2
  136.4 0.0 all-reduce.7.cloned.1.call-update
  136.5 0.9 fusion.38
  137.4 0.0 all-gather.9.cloned.1.call-done
  137.4 108.6 %all-reduce.7.cloned.1.call-done = f32[512,256]{1,0:T(8,128)} async-done(((f32[512,256]{1,0:T(8,128)}), f32[512,256]{1,0:T(8,128)}) %all-reduce.7.cloned.1.call-update) | async-done | bytes 524304 | tf_op jit(solution)/shard_map/psum | solution.py:65
  246.1 7.5 %fusion.23 = f32[1536,256]{1,0:T(8,128)S(1)} fusion(f32[1536,256]{1,0:T(8,128)S(1)} %fusion.38, f32[512,256]{1,0:T(8,128)} %all-reduce.7.cloned.1.call-done, f32[1,512,1536]{2,1,0:T(8,128)} %all-gather.9.cloned.1.call-done, pred[1536]{0:T(1024)(128)(4,1)S(1)} %broadcast_compare_fusion.1), kind=kOutput, calls=%fused_computation.17 | convolution fusion | flops 2416705536 | bytes 6817280 | tf_op jit(solution)/shard_map/dot_general | solution.py:66
  253.5 0.9 fusion.36
  254.5 28.3 %all_to_all.32 = f32[16,96,256]{2,1,0:T(8,128)} all-to-all(f32[16,96,256]{2,1,0:T(8,128)S(1)} %bitcast.61), channel_id=1, replica_groups=mesh['rows'=16,'cols'=16] {'cols'}, dimensions={0} | all-to-all | bytes 3145728 | tf_op jit(solution)/shard_map/all_to_all | solution.py:80
  282.8 6.9 %all-to-all-start.1 = ((f32[96,16,256]{2,0,1:T(8,128)}), f32[96,16,256]{2,0,1:T(8,128)S(1)}, u32[]{:S(2)}, u32[]{:S(2)}) async-start(f32[96,16,256]{2,0,1:T(8,128)} %bitcast.7), calls=%async_computation.1 | async-start | bytes 3145728 | tf_op jit(solution)/shard_map/all_to_all | solution.py:79
  289.7 0.2 all-reduce.9.cloned.1.call-start
  289.9 2.7 fusion.56
  292.6 35.5 %all-to-all-done.1 = f32[96,16,256]{2,0,1:T(8,128)S(1)} async-done(((f32[96,16,256]{2,0,1:T(8,128)}), f32[96,16,256]{2,0,1:T(8,128)S(1)}, u32[]{:S(2)}, u32[]{:S(2)}) %all-to-all-start.1) | async-done | bytes 1572896 | tf_op jit(solution)/shard_map/all_to_all | solution.py:79
  328.1 4.5 convolution_select_fusion.1
  332.6 0.0 copy-start.3
  332.6 0.0 all-reduce.9.cloned.1.call-update
  332.7 0.0 all-reduce.11.cloned.1.call-start
  332.7 0.7 copy-done.3
  333.5 19.8 %all-gather.2 = f32[1,512,256]{2,1,0:T(8,128)} all-gather(f32[1,32,256]{2,1,0:T(8,128)S(1)} %get-tuple-element.12), channel_id=4, replica_groups=mesh['rows'=16,'cols'=16] {'cols'}, dimensions={1}, use_global_device_ids=true | all-gather | bytes 557056 | tf_op jit(solution)/shard_map/all_gather | solution.py:94
  353.2 91.8 %all-reduce.9.cloned.1.call-done = f32[1536,512]{1,0:T(8,128)} async-done(((f32[1536,512]{1,0:T(8,128)}), f32[1536,512]{1,0:T(8,128)}) %all-reduce.9.cloned.1.call-update) | async-done | bytes 3145744 | tf_op jit(solution)/shard_map/psum | solution.py:89
  445.1 0.0 copy-start
  445.1 5.3 fusion.7
  450.3 0.0 copy-done
  450.3 4.5 convolution_select_fusion
  454.8 0.0 all-reduce.11.cloned.1.call-update
  454.9 19.2 %all-gather.3 = f32[1,512,256]{2,1,0:T(8,128)S(1)} all-gather(f32[1,32,256]{2,1,0:T(8,128)S(1)} %get-tuple-element.11), channel_id=5, replica_groups=mesh['rows'=16,'cols'=16] {'cols'}, dimensions={1}, use_global_device_ids=true | all-gather | bytes 557056 | tf_op jit(solution)/shard_map/all_gather | solution.py:94
  474.1 99.3 %all-reduce.11.cloned.1.call-done = f32[1536,512]{1,0:T(8,128)} async-done(((f32[1536,512]{1,0:T(8,128)}), f32[1536,512]{1,0:T(8,128)}) %all-reduce.11.cloned.1.call-update) | async-done | bytes 3145744 | tf_op jit(solution)/shard_map/psum | solution.py:89
  573.4 6.4 %fusion.5 = f32[1536,256]{1,0:T(8,128)} fusion(f32[1536,256]{1,0:T(8,128)S(1)} %fusion.7, f32[1536,512]{1,0:T(8,128)} %all-reduce.11.cloned.1.call-done, s32[]{:T(128)S(6)} %min.16, pred[256]{0:T(512)(128)(4,1)S(1)} %fusion.54, pred[]{:T(512)S(6)} %and.52, f32[1,512,256]{2,1,0:T(8,128)S(1)} %all-gather.3), kind=kOutput, calls=%fused_computation.8 | convolution fusion | flops 2417098752 | bytes 8388869 | tf_op jit(solution)/shard_map/dot_general | solution.py:92
  (5 shorter events, 0.0 us)
Async XLA Ops:
  7.4 119.4 %all-reduce.5.cloned.1.call-start = ((), (), s32[]{:S(2)}) async-start(), calls=%async_computation.2 | async-start | bytes 1048576 | tf_op jit(solution)/shard_map/psum | solution.py:65
  7.4 2.8 copy-start.1
  10.2 1.4 copy-start.2
  11.6 115.2 %all-gather.7.cloned.1.call-start = ((), (), s32[]{:S(2)}) async-start(), calls=%async_computation.6 | async-start | bytes 3342336 | tf_op jit(solution)/shard_map/all_gather | solution.py:67
  12.4 125.0 %all-gather.9.cloned.1.call-start = ((), (), s32[]{:S(2)}) async-start(), calls=%async_computation.7 | async-start | bytes 3342336 | tf_op jit(solution)/shard_map/all_gather | solution.py:67
  13.0 233.1 %all-reduce.7.cloned.1.call-start = ((), (), s32[]{:S(2)}) async-start(), calls=%async_computation.3 | async-start | bytes 1048576 | tf_op jit(solution)/shard_map/psum | solution.py:65
  282.8 45.4 %all-to-all-start.1 = ((f32[96,16,256]{2,0,1:T(8,128)}), f32[96,16,256]{2,0,1:T(8,128)S(1)}, u32[]{:S(2)}, u32[]{:S(2)}) async-start(f32[96,16,256]{2,0,1:T(8,128)} %bitcast.7), calls=%async_computation.1 | async-start | bytes 3145728 | tf_op jit(solution)/shard_map/all_to_all | solution.py:79
  289.7 155.4 %all-reduce.9.cloned.1.call-start = ((), (), s32[]{:S(2)}) async-start(), calls=%async_computation.4 | async-start | bytes 6291456 | tf_op jit(solution)/shard_map/psum | solution.py:89
  332.6 0.8 copy-start.3
  332.7 240.7 %all-reduce.11.cloned.1.call-start = ((), (), s32[]{:S(2)}) async-start(), calls=%async_computation.5 | async-start | bytes 6291456 | tf_op jit(solution)/shard_map/psum | solution.py:89
  445.1 5.3 copy-start
Sparse Core Ops, SparseCore 0:
  11.7 115.0 all-reduce.4
  136.6 109.4 all-reduce.6
  332.8 112.2 all-reduce.8
  455.0 118.3 all-reduce.10
Sparse Core Ops, SparseCore 1:
  14.8 56.3 all-gather.6
  73.4 51.8 all-gather.8
where the time goes:
time: 587 us
  waiting for transfers between devices  450 us (77%)
  blocking collectives  67.2 us (11%)
  matrix products  39.2 us (7%)
  between operations  14.7 us (3%)
  starting transfers between devices  7.32 us (1%)
  local copies, waits for them, and re-layouts  7.02 us (1%)
    psum x2, waiting for transfers between devices, on_device(): solved = lax.psum(jnp.where(member, partial_value, 0.0), 'rows')  222 us
    psum x2, waiting for transfers between devices, total_rows(): return lax.psum(partial_sum, 'rows')  191 us
    all_gather x2, blocking collectives, update_rows(): lax.all_gather(second_factor[panel_number], 'cols', axis=0, tiled=True)  38.9 us
    all_to_all x1, waiting for transfers between devices, on_device(): lax.all_to_all(lax.all_to_all(current, 'cols', split_axis=0, concat_axis=...  35.5 us
    all_to_all x1, blocking collectives, on_device(): lax.all_to_all(current, 'cols', split_axis=0, concat_axis=1, tiled=True)  28.3 us
    dot_general x2, matrix products, on_device(): lax.dot_general(lax.all_gather(first_factor[panel_index], 'cols', axis=0,...  14.7 us
  transfers between devices with their start and end apart: 7, of which 5 were waited for; matrix products, arithmetic and copies ran while one was open for 2% of the time, Pallas kernels for 0%

commit v1 on v0

--- a/solution.py
+++ b/solution.py
@@ -7,6 +7,24 @@
 HIGHEST = lax.Precision.HIGHEST
 CONTRACT_ROWS = (((0,), (0,)), ((), ()))
 CONTRACT_COLS = (((1,), (1,)), ((), ()))
+
+
+def gather_around(shard, axis, dim):
+    ways, here, hop = (lax.axis_size(axis), lax.axis_index(axis), shard.shape[dim])
+    dims = [n * ways if d == dim else n for d, n in enumerate(shard.shape)]
+    full = lax.dynamic_update_slice_in_dim(
+        jnp.zeros(dims, shard.dtype), shard, here * hop, axis=dim
+    )
+    going_up = going_down = shard
+    for far in range(1, ways // 2 + 1):
+        going_up = lax.ppermute(going_up, axis, [(d, (d + 1) % ways) for d in range(ways)])
+        full = lax.dynamic_update_slice_in_dim(full, going_up, (here - far) % ways * hop, axis=dim)
+        if 2 * far < ways:
+            going_down = lax.ppermute(going_down, axis, [(d, (d - 1) % ways) for d in range(ways)])
+            full = lax.dynamic_update_slice_in_dim(
+                full, going_down, (here + far) % ways * hop, axis=dim
+            )
+    return full
 
 
 def right_solve(current, first_column, inverses, total_of, update_of):
@@ -91,7 +109,7 @@
     def update_rows(panel_number, solved_cols):
         return jnp.dot(
             solved_cols,
-            lax.all_gather(second_factor[panel_number], "cols", axis=0, tiled=True),
+            gather_around(second_factor[panel_number], "cols", 0),
             precision=HIGHEST,
             preferred_element_type=jnp.float32,
         )

time: 587 us -> 597 us (1.017); the launches traced: 587 us -> 588 us
  starting transfers between devices: 7.32 us -> 75.1 us
  waiting for transfers between devices: 450 us -> 411 us
  blocking collectives: 67.2 us -> 28.3 us
  local copies, waits for them, and re-layouts: 7.02 us -> 17.3 us
    ppermute x0 -> x30, starting transfers between devices: none -> 67.8 us  [the longest x14 65.2 us: gather_around(): lax.ppermute(going_down, axis, [(d, (d - 1) % ways) for d in range(ways)])]
    all_gather x2 -> x0, blocking collectives: 38.9 us -> none  [update_rows(): lax.all_gather(second_factor[panel_number], 'cols', axis=0, tiled=True)]
    psum x2, waiting for transfers between devices: 191 us -> 154 us  [total_rows(): return lax.psum(partial_sum, 'rows')]
    all_to_all x1, waiting for transfers between devices: 35.5 us -> 14.7 us  [on_device(): lax.all_to_all(lax.all_to_all(current, 'cols', split_axis=0, concat_axis=...]
    ppermute x0 -> x30, waiting for transfers between devices: none -> 18.4 us  [the longest x16 18.4 us: gather_around(): lax.ppermute(going_up, axis, [(d, (d + 1) % ways) for d in range(ways)])]
    dynamic_update_slice x0 -> x32, local copies, waits for them, and re-layouts: none -> 9.15 us  [the longest x16 4.87 us: gather_around(): lax.dynamic_update_slice_in_dim(full, going_up, (here - far) % ways * hop...]
  transfers between devices with their start and end apart: 7 -> 37, of which waited for: 5 -> 17; matrix products, arithmetic and copies ran while one was open for 2% -> 6% of each run, Pallas kernels for 0% -> 0%
where the time goes in v1:
time: 597 us; the launch traced here: 588 us
  waiting for transfers between devices  411 us (69%)
  starting transfers between devices  75.1 us (13%)
  matrix products  39.1 us (7%)
  blocking collectives  28.3 us (5%)
  local copies, waits for them, and re-layouts  17.3 us (3%)
  between operations  15.3 us (3%)
    psum x2, waiting for transfers between devices, on_device(): solved = lax.psum(jnp.where(member, partial_value, 0.0), 'rows')  222 us
    psum x2, waiting for transfers between devices, total_rows(): return lax.psum(partial_sum, 'rows')  154 us
    ppermute x14, starting transfers between devices, gather_around(): lax.ppermute(going_down, axis, [(d, (d - 1) % ways) for d in range(ways)])  65.2 us
    all_to_all x1, blocking collectives, on_device(): lax.all_to_all(current, 'cols', split_axis=0, concat_axis=1, tiled=True)  28.3 us
    ppermute x16, waiting for transfers between devices, gather_around(): lax.ppermute(going_up, axis, [(d, (d + 1) % ways) for d in range(ways)])  18.4 us
    dot_general x2, matrix products, on_device(): lax.dot_general(lax.all_gather(first_factor[panel_index], 'cols', axis=0,...  14.7 us
    all_to_all x1, waiting for transfers between devices, on_device(): lax.all_to_all(lax.all_to_all(current, 'cols', split_axis=0, concat_axis=...  14.7 us
  transfers between devices with their start and end apart: 37, of which 17 were waited for; matrix products, arithmetic and copies ran while one was open for 6% of the time, Pallas kernels for 0%

profile of v1, /device:TPU:1, one launch (start us, length us, event | category | flops | bytes accessed | tf_op | source)
XLA Modules:
  0.0 587.7 jit_solution(6294393598763280376)
XLA Ops:
  7.4 2.8 fusion.55
  10.2 1.4 convolution_select_fusion.3
  11.6 0.8 fusion.56
  12.5 0.5 all-gather.7.cloned.1.call-update
  13.1 113.7 %all-reduce.5.cloned.1.call-done = f32[512,256]{1,0:T(8,128)} async-done(((f32[512,256]{1,0:T(8,128)}), f32[512,256]{1,0:T(8,128)}) %all-reduce.5.cloned.1.call-update) | async-done | bytes 524304 | tf_op jit(solution)/shard_map/psum | solution.py:83
  126.9 7.2 %fusion.14 = f32[1536,256]{1,0:T(8,128)S(1)} fusion(f32[1536,256]{1,0:T(8,128)S(1)} %copy-done.4, f32[512,256]{1,0:T(8,128)} %all-reduce.5.cloned.1.call-done, f32[1,512,1536]{2,1,0:T(8,128)} %all-gather.5.cloned.1.call-done, pred[1536]{0:T(1024)(128)(4,1)S(1)} %broadcast_compare_fusion), kind=kOutput, calls=%fused_computation.14 | convolution fusion | flops 2416705536 | bytes 6817280 | tf_op jit(solution)/shard_map/dot_general | solution.py:84
  134.1 2.4 convolution_select_fusion.2
  136.5 0.9 fusion.36
  137.5 108.8 %all-reduce.7.cloned.1.call-done = f32[512,256]{1,0:T(8,128)} async-done(((f32[512,256]{1,0:T(8,128)}), f32[512,256]{1,0:T(8,128)}) %all-reduce.7.cloned.1.call-update) | async-done | bytes 524304 | tf_op jit(solution)/shard_map/psum | solution.py:83
  246.3 7.5 %fusion.23 = f32[1536,256]{1,0:T(8,128)S(1)} fusion(f32[1536,256]{1,0:T(8,128)S(1)} %fusion.36, f32[512,256]{1,0:T(8,128)} %all-reduce.7.cloned.1.call-done, f32[1,512,1536]{2,1,0:T(8,128)} %all-gather.7.cloned.1.call-done, pred[1536]{0:T(1024)(128)(4,1)S(1)} %broadcast_compare_fusion.1), kind=kOutput, calls=%fused_computation.17 | convolution fusion | flops 2416705536 | bytes 6817280 | tf_op jit(solution)/shard_map/dot_general | solution.py:84
  253.7 0.9 fusion.34
  254.7 28.3 %all_to_all.32 = f32[16,96,256]{2,1,0:T(8,128)} all-to-all(f32[16,96,256]{2,1,0:T(8,128)S(1)} %bitcast.65), channel_id=1, replica_groups=mesh['rows'=16,'cols'=16] {'cols'}, dimensions={0} | all-to-all | bytes 3145728 | tf_op jit(solution)/shard_map/all_to_all | solution.py:98
  282.9 7.1 %all-to-all-start.1 = ((f32[96,16,256]{2,0,1:T(8,128)}), f32[96,16,256]{2,0,1:T(8,128)S(1)}, u32[]{:S(2)}, u32[]{:S(2)}) async-start(f32[96,16,256]{2,0,1:T(8,128)} %bitcast.7), calls=%async_computation.1 | async-start | bytes 3145728 | tf_op jit(solution)/shard_map/all_to_all | solution.py:97
  290.1 0.6 collective-permute-start
  290.6 4.5 collective-permute-start.1
  295.1 4.8 collective-permute-start.16
  300.0 0.7 copy-done.3
  300.8 2.7 fusion.54
  303.6 4.8 collective-permute-start.3
  308.4 4.8 collective-permute-start.18
  313.1 0.6 constant_dynamic-update-slice_fusion.28
  313.8 14.7 %all-to-all-done.1 = f32[96,16,256]{2,0,1:T(8,128)S(1)} async-done(((f32[96,16,256]{2,0,1:T(8,128)}), f32[96,16,256]{2,0,1:T(8,128)S(1)}, u32[]{:S(2)}, u32[]{:S(2)}) %all-to-all-start.1) | async-done | bytes 1572896 | tf_op jit(solution)/shard_map/all_to_all | solution.py:97
  328.4 4.5 convolution_select_fusion.1
  333.0 0.6 constant_dynamic-update-slice_fusion.27
  333.6 0.3 collective-permute-start.4
  333.9 4.5 collective-permute-start.5
  338.4 0.6 constant_dynamic-update-slice_fusion.26
  339.0 0.6 constant_dynamic-update-slice_fusion.25
  339.6 0.7 collective-permute-done.4
  340.3 4.8 collective-permute-start.7
  345.1 0.6 constant_dynamic-update-slice_fusion.24
  345.7 0.6 constant_dynamic-update-slice_fusion.23
  346.6 4.8 collective-permute-start.9
  351.4 0.6 constant_dynamic-update-slice_fusion.22
  352.0 0.6 constant_dynamic-update-slice_fusion.21
  352.7 4.8 collective-permute-start.11
  357.5 0.6 constant_dynamic-update-slice_fusion.20
  358.1 0.6 constant_dynamic-update-slice_fusion.19
  358.8 4.8 collective-permute-start.13
  363.6 0.6 constant_dynamic-update-slice_fusion.18
  364.2 0.6 constant_dynamic-update-slice_fusion.17
  364.9 0.6 constant_dynamic-update-slice_fusion.16
  365.5 0.6 constant_dynamic-update-slice_fusion.15
  366.1 4.9 collective-permute-done.14
  370.9 0.6 constant_dynamic-update-slice_fusion.14
  371.5 73.8 %all-reduce.9.cloned.1.call-done = f32[1536,512]{1,0:T(8,128)} async-done(((f32[1536,512]{1,0:T(8,128)}), f32[1536,512]{1,0:T(8,128)}) %all-reduce.9.cloned.1.call-update) | async-done | bytes 3145744 | tf_op jit(solution)/shard_map/psum | solution.py:107
  445.4 5.3 fusion.7
  450.6 4.5 convolution_select_fusion
  455.2 1.0 copy-done.2
  456.2 1.3 collective-permute-start.19
  457.5 3.6 collective-permute-start.20
  461.1 1.3 collective-permute-done.19
  462.4 0.2 collective-permute-start.21
  462.6 4.8 collective-permute-start.22
  467.4 1.3 collective-permute-done.21
  468.7 4.8 collective-permute-start.24
  473.5 1.3 collective-permute-done.23
  474.8 4.8 collective-permute-start.26
  479.6 1.3 collective-permute-done.25
  480.9 4.8 collective-permute-start.28
  485.6 1.3 collective-permute-done.27
  487.0 6.0 %collective-permute-done.29 = f32[32,256]{1,0:T(8,128)S(1)} collective-permute-done((f32[32,256]{1,0:T(8,128)S(1)}, f32[32,256]{1,0:T(8,128)S(1)}, u32[]{:S(2)}, u32[]{:S(2)}) %collective-permute-start.29) | collective-permute-done | bytes 32800 | tf_op jit(solution)/shard_map/ppermute | solution.py:20
  493.0 80.7 %all-reduce.11.cloned.1.call-done = f32[1536,512]{1,0:T(8,128)} async-done(((f32[1536,512]{1,0:T(8,128)}), f32[1536,512]{1,0:T(8,128)}) %all-reduce.11.cloned.1.call-update) | async-done | bytes 3145744 | tf_op jit(solution)/shard_map/psum | solution.py:107
  573.7 6.4 %fusion.5 = f32[1536,256]{1,0:T(8,128)} fusion(f32[1536,256]{1,0:T(8,128)S(1)} %fusion.7, f32[1536,512]{1,0:T(8,128)} %all-reduce.11.cloned.1.call-done, f32[512,256]{1,0:T(8,128)S(1)} %constant_dynamic-update-slice_fusion.30, s32[]{:T(128)S(6)} %min.16, pred[256]{0:T(512)(128)(4,1)S(1)} %fusion.52, pred[]{:T(512)S(6)} %and.129), kind=kOutput, calls=%fused_computation.8 | convolution fusion | flops 2417098752 | bytes 8388869 | tf_op jit(solution)/shard_map/dot_general | solution.py:110
  (83 shorter events, 1.2 us)
Async XLA Ops:
  7.4 119.5 %all-reduce.5.cloned.1.call-start = ((), (), s32[]{:S(2)}) async-start(), calls=%async_computation.2 | async-start | bytes 1048576 | tf_op jit(solution)/shard_map/psum | solution.py:83
  7.4 2.8 copy-start.4
  10.2 1.4 copy-start.5
  11.6 115.3 %all-gather.5.cloned.1.call-start = ((), (), s32[]{:S(2)}) async-start(), calls=%async_computation.6 | async-start | bytes 3342336 | tf_op jit(solution)/shard_map/all_gather | solution.py:85
  12.5 125.0 %all-gather.7.cloned.1.call-start = ((), (), s32[]{:S(2)}) async-start(), calls=%async_computation.7 | async-start | bytes 3342336 | tf_op jit(solution)/shard_map/all_gather | solution.py:85
  13.1 233.2 %all-reduce.7.cloned.1.call-start = ((), (), s32[]{:S(2)}) async-start(), calls=%async_computation.3 | async-start | bytes 1048576 | tf_op jit(solution)/shard_map/psum | solution.py:83
  282.9 7.1 %copy-start.6 = (f32[2,32,256]{2,1,0:T(8,128)S(1)}, f32[2,32,256]{2,1,0:T(8,128)}, u32[]{:S(2)}) copy-start(f32[2,32,256]{2,1,0:T(8,128)} %param.9) | copy-start | bytes 196612
  282.9 45.5 %all-to-all-start.1 = ((f32[96,16,256]{2,0,1:T(8,128)}), f32[96,16,256]{2,0,1:T(8,128)S(1)}, u32[]{:S(2)}, u32[]{:S(2)}) async-start(f32[96,16,256]{2,0,1:T(8,128)} %bitcast.7), calls=%async_computation.1 | async-start | bytes 3145728 | tf_op jit(solution)/shard_map/all_to_all | solution.py:97
  290.0 155.4 %all-reduce.9.cloned.1.call-start = ((), (), s32[]{:S(2)}) async-start(), calls=%async_computation.4 | async-start | bytes 6291456 | tf_op jit(solution)/shard_map/psum | solution.py:107
  290.1 13.4 %collective-permute-start = (f32[32,256]{1,0:T(8,128)S(1)}, f32[32,256]{1,0:T(8,128)S(1)}, u32[]{:S(2)}, u32[]{:S(2)}) collective-permute-start(f32[32,256]{1,0:T(8,128)S(1)} %get-tuple-element.12), channel_id=1, source_target_pairs={{0,1},{1,2},{2,3},{3,4},{4,5},{5,6},{6,7},{7,8},{8,9},{9,10},{10,1... | collective-permute-start | bytes 98312 | tf_op jit(solution)/shard_map/ppermute | solution.py:20
  290.6 12.9 %collective-permute-start.1 = (f32[32,256]{1,0:T(8,128)S(1)}, f32[32,256]{1,0:T(8,128)S(1)}, u32[]{:S(2)}, u32[]{:S(2)}) collective-permute-start(f32[32,256]{1,0:T(8,128)S(1)} %get-tuple-element.12), channel_id=1, source_target_pairs={{0,15},{1,0},{2,1},{3,2},{4,3},{5,4},{6,5},{7,6},{8,7},{9,8},{10,9... | collective-permute-start | bytes 98312 | tf_op jit(solution)/shard_map/ppermute | solution.py:23
  295.1 13.2 %collective-permute-start.15 = (f32[32,256]{1,0:T(8,128)S(1)}, f32[32,256]{1,0:T(8,128)S(1)}, u32[]{:S(2)}, u32[]{:S(2)}) collective-permute-start(f32[32,256]{1,0:T(8,128)S(1)} %get-tuple-element.11), channel_id=1, source_target_pairs={{0,1},{1,2},{2,3},{3,4},{4,5},{5,6},{6,7},{7,8},{8,9},{9,10},{10,1... | collective-permute-start | bytes 98312 | tf_op jit(solution)/shard_map/ppermute | solution.py:20
  295.1 13.2 %collective-permute-start.16 = (f32[32,256]{1,0:T(8,128)S(1)}, f32[32,256]{1,0:T(8,128)S(1)}, u32[]{:S(2)}, u32[]{:S(2)}) collective-permute-start(f32[32,256]{1,0:T(8,128)S(1)} %get-tuple-element.11), channel_id=1, source_target_pairs={{0,15},{1,0},{2,1},{3,2},{4,3},{5,4},{6,5},{7,6},{8,7},{9,8},{10,9... | collective-permute-start | bytes 98312 | tf_op jit(solution)/shard_map/ppermute | solution.py:23
  300.0 0.8 copy-start.3
  303.5 30.1 %collective-permute-start.2 = (f32[32,256]{1,0:T(8,128)S(1)}, f32[32,256]{1,0:T(8,128)S(1)}, u32[]{:S(2)}, u32[]{:S(2)}) collective-permute-start(f32[32,256]{1,0:T(8,128)S(1)} %collective-permute-done), channel_id=1, source_target_pairs={{0,1},{1,2},{2,3},{3,4},{4,5},{5,6},{6,7},{7,8},{8,9},{9,10},{10,1... | collective-permute-start | bytes 98312 | tf_op jit(solution)/shard_map/ppermute | solution.py:20
  303.6 30.3 %collective-permute-start.3 = (f32[32,256]{1,0:T(8,128)S(1)}, f32[32,256]{1,0:T(8,128)S(1)}, u32[]{:S(2)}, u32[]{:S(2)}) collective-permute-start(f32[32,256]{1,0:T(8,128)S(1)} %collective-permute-done.1), channel_id=1, source_target_pairs={{0,15},{1,0},{2,1},{3,2},{4,3},{5,4},{6,5},{7,6},{8,7},{9,8},{10,9... | collective-permute-start | bytes 98312 | tf_op jit(solution)/shard_map/ppermute | solution.py:23
  308.3 147.9 %collective-permute-start.17 = (f32[32,256]{1,0:T(8,128)S(1)}, f32[32,256]{1,0:T(8,128)S(1)}, u32[]{:S(2)}, u32[]{:S(2)}) collective-permute-start(f32[32,256]{1,0:T(8,128)S(1)} %collective-permute-done.15), channel_id=1, source_target_pairs={{0,1},{1,2},{2,3},{3,4},{4,5},{5,6},{6,7},{7,8},{8,9},{9,10},{10,1... | collective-permute-start | bytes 98312 | tf_op jit(solution)/shard_map/ppermute | solution.py:20
  308.4 149.1 %collective-permute-start.18 = (f32[32,256]{1,0:T(8,128)S(1)}, f32[32,256]{1,0:T(8,128)S(1)}, u32[]{:S(2)}, u32[]{:S(2)}) collective-permute-start(f32[32,256]{1,0:T(8,128)S(1)} %collective-permute-done.16), channel_id=1, source_target_pairs={{0,15},{1,0},{2,1},{3,2},{4,3},{5,4},{6,5},{7,6},{8,7},{9,8},{10,9... | collective-permute-start | bytes 98312 | tf_op jit(solution)/shard_map/ppermute | solution.py:23
  313.7 19.2 %copy-start.1 = (f32[512,256]{1,0:T(8,128)}, f32[512,256]{1,0:T(8,128)S(1)}, u32[]{:S(2)}) copy-start(f32[512,256]{1,0:T(8,128)S(1)} %constant_dynamic-update-slice_fusion.12) | copy-start | bytes 1572868
  333.0 240.7 %all-reduce.11.cloned.1.call-start = ((), (), s32[]{:S(2)}) async-start(), calls=%async_computation.5 | async-start | bytes 6291456 | tf_op jit(solution)/shard_map/psum | solution.py:107
  333.6 6.7 %collective-permute-start.4 = (f32[32,256]{1,0:T(8,128)S(1)}, f32[32,256]{1,0:T(8,128)S(1)}, u32[]{:S(2)}, u32[]{:S(2)}) collective-permute-start(f32[32,256]{1,0:T(8,128)S(1)} %collective-permute-done.2), channel_id=1, source_target_pairs={{0,1},{1,2},{2,3},{3,4},{4,5},{5,6},{6,7},{7,8},{8,9},{9,10},{10,1... | collective-permute-start | bytes 98312 | tf_op jit(solution)/shard_map/ppermute | solution.py:20
  333.9 6.4 %collective-permute-start.5 = (f32[32,256]{1,0:T(8,128)S(1)}, f32[32,256]{1,0:T(8,128)S(1)}, u32[]{:S(2)}, u32[]{:S(2)}) collective-permute-start(f32[32,256]{1,0:T(8,128)S(1)} %collective-permute-done.3), channel_id=1, source_target_pairs={{0,15},{1,0},{2,1},{3,2},{4,3},{5,4},{6,5},{7,6},{8,7},{9,8},{10,9... | collective-permute-start | bytes 98312 | tf_op jit(solution)/shard_map/ppermute | solution.py:23
  340.3 6.1 %collective-permute-start.6 = (f32[32,256]{1,0:T(8,128)S(1)}, f32[32,256]{1,0:T(8,128)S(1)}, u32[]{:S(2)}, u32[]{:S(2)}) collective-permute-start(f32[32,256]{1,0:T(8,128)S(1)} %collective-permute-done.4), channel_id=1, source_target_pairs={{0,1},{1,2},{2,3},{3,4},{4,5},{5,6},{6,7},{7,8},{8,9},{9,10},{10,1... | collective-permute-start | bytes 98312 | tf_op jit(solution)/shard_map/ppermute | solution.py:20
  340.3 6.3 %collective-permute-start.7 = (f32[32,256]{1,0:T(8,128)S(1)}, f32[32,256]{1,0:T(8,128)S(1)}, u32[]{:S(2)}, u32[]{:S(2)}) collective-permute-start(f32[32,256]{1,0:T(8,128)S(1)} %collective-permute-done.5), channel_id=1, source_target_pairs={{0,15},{1,0},{2,1},{3,2},{4,3},{5,4},{6,5},{7,6},{8,7},{9,8},{10,9... | collective-permute-start | bytes 98312 | tf_op jit(solution)/shard_map/ppermute | solution.py:23
  346.4 6.3 %collective-permute-start.8 = (f32[32,256]{1,0:T(8,128)S(1)}, f32[32,256]{1,0:T(8,128)S(1)}, u32[]{:S(2)}, u32[]{:S(2)}) collective-permute-start(f32[32,256]{1,0:T(8,128)S(1)} %collective-permute-done.6), channel_id=1, source_target_pairs={{0,1},{1,2},{2,3},{3,4},{4,5},{5,6},{6,7},{7,8},{8,9},{9,10},{10,1... | collective-permute-start | bytes 98312 | tf_op jit(solution)/shard_map/ppermute | solution.py:20
  346.6 6.1 %collective-permute-start.9 = (f32[32,256]{1,0:T(8,128)S(1)}, f32[32,256]{1,0:T(8,128)S(1)}, u32[]{:S(2)}, u32[]{:S(2)}) collective-permute-start(f32[32,256]{1,0:T(8,128)S(1)} %collective-permute-done.7), channel_id=1, source_target_pairs={{0,15},{1,0},{2,1},{3,2},{4,3},{5,4},{6,5},{7,6},{8,7},{9,8},{10,9... | collective-permute-start | bytes 98312 | tf_op jit(solution)/shard_map/ppermute | solution.py:23
  352.7 6.1 %collective-permute-start.10 = (f32[32,256]{1,0:T(8,128)S(1)}, f32[32,256]{1,0:T(8,128)S(1)}, u32[]{:S(2)}, u32[]{:S(2)}) collective-permute-start(f32[32,256]{1,0:T(8,128)S(1)} %collective-permute-done.8), channel_id=1, source_target_pairs={{0,1},{1,2},{2,3},{3,4},{4,5},{5,6},{6,7},{7,8},{8,9},{9,10},{10,1... | collective-permute-start | bytes 98312 | tf_op jit(solution)/shard_map/ppermute | solution.py:20
  352.7 6.1 %collective-permute-start.11 = (f32[32,256]{1,0:T(8,128)S(1)}, f32[32,256]{1,0:T(8,128)S(1)}, u32[]{:S(2)}, u32[]{:S(2)}) collective-permute-start(f32[32,256]{1,0:T(8,128)S(1)} %collective-permute-done.9), channel_id=1, source_target_pairs={{0,15},{1,0},{2,1},{3,2},{4,3},{5,4},{6,5},{7,6},{8,7},{9,8},{10,9... | collective-permute-start | bytes 98312 | tf_op jit(solution)/shard_map/ppermute | solution.py:23
  358.8 6.1 %collective-permute-start.12 = (f32[32,256]{1,0:T(8,128)S(1)}, f32[32,256]{1,0:T(8,128)S(1)}, u32[]{:S(2)}, u32[]{:S(2)}) collective-permute-start(f32[32,256]{1,0:T(8,128)S(1)} %collective-permute-done.10), channel_id=1, source_target_pairs={{0,1},{1,2},{2,3},{3,4},{4,5},{5,6},{6,7},{7,8},{8,9},{9,10},{10,1... | collective-permute-start | bytes 98312 | tf_op jit(solution)/shard_map/ppermute | solution.py:20
  358.8 6.7 %collective-permute-start.13 = (f32[32,256]{1,0:T(8,128)S(1)}, f32[32,256]{1,0:T(8,128)S(1)}, u32[]{:S(2)}, u32[]{:S(2)}) collective-permute-start(f32[32,256]{1,0:T(8,128)S(1)} %collective-permute-done.11), channel_id=1, source_target_pairs={{0,15},{1,0},{2,1},{3,2},{4,3},{5,4},{6,5},{7,6},{8,7},{9,8},{10,9... | collective-permute-start | bytes 98312 | tf_op jit(solution)/shard_map/ppermute | solution.py:23
  364.8 6.1 %collective-permute-start.14 = (f32[32,256]{1,0:T(8,128)S(1)}, f32[32,256]{1,0:T(8,128)S(1)}, u32[]{:S(2)}, u32[]{:S(2)}) collective-permute-start(f32[32,256]{1,0:T(8,128)S(1)} %collective-permute-done.12), channel_id=1, source_target_pairs={{0,1},{1,2},{2,3},{3,4},{4,5},{5,6},{6,7},{7,8},{8,9},{9,10},{10,1... | collective-permute-start | bytes 98312 | tf_op jit(solution)/shard_map/ppermute | solution.py:20
  445.4 5.3 copy-start
  455.1 1.0 copy-start.2
  456.2 6.2 %collective-permute-start.19 = (f32[32,256]{1,0:T(8,128)S(1)}, f32[32,256]{1,0:T(8,128)S(1)}, u32[]{:S(2)}, u32[]{:S(2)}) collective-permute-start(f32[32,256]{1,0:T(8,128)S(1)} %collective-permute-done.17), channel_id=1, source_target_pairs={{0,1},{1,2},{2,3},{3,4},{4,5},{5,6},{6,7},{7,8},{8,9},{9,10},{10,1... | collective-permute-start | bytes 98312 | tf_op jit(solution)/shard_map/ppermute | solution.py:20
  457.5 5.1 collective-permute-start.20
  462.4 6.3 %collective-permute-start.21 = (f32[32,256]{1,0:T(8,128)S(1)}, f32[32,256]{1,0:T(8,128)S(1)}, u32[]{:S(2)}, u32[]{:S(2)}) collective-permute-start(f32[32,256]{1,0:T(8,128)S(1)} %collective-permute-done.19), channel_id=1, source_target_pairs={{0,1},{1,2},{2,3},{3,4},{4,5},{5,6},{6,7},{7,8},{8,9},{9,10},{10,1... | collective-permute-start | bytes 98312 | tf_op jit(solution)/shard_map/ppermute | solution.py:20
  462.6 6.1 %collective-permute-start.22 = (f32[32,256]{1,0:T(8,128)S(1)}, f32[32,256]{1,0:T(8,128)S(1)}, u32[]{:S(2)}, u32[]{:S(2)}) collective-permute-start(f32[32,256]{1,0:T(8,128)S(1)} %collective-permute-done.20), channel_id=1, source_target_pairs={{0,15},{1,0},{2,1},{3,2},{4,3},{5,4},{6,5},{7,6},{8,7},{9,8},{10,9... | collective-permute-start | bytes 98312 | tf_op jit(solution)/shard_map/ppermute | solution.py:23
  468.7 6.1 %collective-permute-start.23 = (f32[32,256]{1,0:T(8,128)S(1)}, f32[32,256]{1,0:T(8,128)S(1)}, u32[]{:S(2)}, u32[]{:S(2)}) collective-permute-start(f32[32,256]{1,0:T(8,128)S(1)} %collective-permute-done.21), channel_id=1, source_target_pairs={{0,1},{1,2},{2,3},{3,4},{4,5},{5,6},{6,7},{7,8},{8,9},{9,10},{10,1... | collective-permute-start | bytes 98312 | tf_op jit(solution)/shard_map/ppermute | solution.py:20
  468.7 6.1 %collective-permute-start.24 = (f32[32,256]{1,0:T(8,128)S(1)}, f32[32,256]{1,0:T(8,128)S(1)}, u32[]{:S(2)}, u32[]{:S(2)}) collective-permute-start(f32[32,256]{1,0:T(8,128)S(1)} %collective-permute-done.22), channel_id=1, source_target_pairs={{0,15},{1,0},{2,1},{3,2},{4,3},{5,4},{6,5},{7,6},{8,7},{9,8},{10,9... | collective-permute-start | bytes 98312 | tf_op jit(solution)/shard_map/ppermute | solution.py:23
  474.8 6.1 %collective-permute-start.25 = (f32[32,256]{1,0:T(8,128)S(1)}, f32[32,256]{1,0:T(8,128)S(1)}, u32[]{:S(2)}, u32[]{:S(2)}) collective-permute-start(f32[32,256]{1,0:T(8,128)S(1)} %collective-permute-done.23), channel_id=1, source_target_pairs={{0,1},{1,2},{2,3},{3,4},{4,5},{5,6},{6,7},{7,8},{8,9},{9,10},{10,1... | collective-permute-start | bytes 98312 | tf_op jit(solution)/shard_map/ppermute | solution.py:20
  474.8 6.1 %collective-permute-start.26 = (f32[32,256]{1,0:T(8,128)S(1)}, f32[32,256]{1,0:T(8,128)S(1)}, u32[]{:S(2)}, u32[]{:S(2)}) collective-permute-start(f32[32,256]{1,0:T(8,128)S(1)} %collective-permute-done.24), channel_id=1, source_target_pairs={{0,15},{1,0},{2,1},{3,2},{4,3},{5,4},{6,5},{7,6},{8,7},{9,8},{10,9... | collective-permute-start | bytes 98312 | tf_op jit(solution)/shard_map/ppermute | solution.py:23
  480.8 6.1 %collective-permute-start.27 = (f32[32,256]{1,0:T(8,128)S(1)}, f32[32,256]{1,0:T(8,128)S(1)}, u32[]{:S(2)}, u32[]{:S(2)}) collective-permute-start(f32[32,256]{1,0:T(8,128)S(1)} %collective-permute-done.25), channel_id=1, source_target_pairs={{0,1},{1,2},{2,3},{3,4},{4,5},{5,6},{6,7},{7,8},{8,9},{9,10},{10,1... | collective-permute-start | bytes 98312 | tf_op jit(solution)/shard_map/ppermute | solution.py:20
  480.9 6.1 %collective-permute-start.28 = (f32[32,256]{1,0:T(8,128)S(1)}, f32[32,256]{1,0:T(8,128)S(1)}, u32[]{:S(2)}, u32[]{:S(2)}) collective-permute-start(f32[32,256]{1,0:T(8,128)S(1)} %collective-permute-done.26), channel_id=1, source_target_pairs={{0,15},{1,0},{2,1},{3,2},{4,3},{5,4},{6,5},{7,6},{8,7},{9,8},{10,9... | collective-permute-start | bytes 98312 | tf_op jit(solution)/shard_map/ppermute | solution.py:23
  486.9 6.1 %collective-permute-start.29 = (f32[32,256]{1,0:T(8,128)S(1)}, f32[32,256]{1,0:T(8,128)S(1)}, u32[]{:S(2)}, u32[]{:S(2)}) collective-permute-start(f32[32,256]{1,0:T(8,128)S(1)} %collective-permute-done.27), channel_id=1, source_target_pairs={{0,1},{1,2},{2,3},{3,4},{4,5},{5,6},{6,7},{7,8},{8,9},{9,10},{10,1... | collective-permute-start | bytes 98312 | tf_op jit(solution)/shard_map/ppermute | solution.py:20
Sparse Core Ops, SparseCore 0:
  11.7 115.1 all-reduce.4
  136.6 109.5 all-reduce.6
  333.1 112.2 all-reduce.8
  455.3 118.3 all-reduce.10
Sparse Core Ops, SparseCore 1:
  14.8 56.2 all-gather.4
  73.4 51.8 all-gather.6
